TPU v7x, 32 devices: a whole 2x2x4 slice. The times are simulated.
32 devices in a mesh: seg: 4 (over z), blk: 8 (over y, x, core).
Axes of the slice: x: 2, y: 2, z: 4, core: 2. Of those that a mesh axis runs over, the one named last changes fastest.
Arguments:
- train_acts: bfloat16 [4, 1024, 512], P('seg', 'blk'), may hold values from -6 to 6
- train_grads: bfloat16 [4, 1024, 4096], P('seg', 'blk'), may hold values from -0.0059814453 to 0.0059814453
- counts: int32 [8], replicated, may hold values from 1 to 2, as said below
- basis_in: bfloat16 [4, 1, 512, 512], P('seg'), may hold values from -1 to 1, as said below
- basis_out: bfloat16 [4, 8, 512, 512], P('seg', 'blk'), may hold values from -1 to 1, as said below
- eigenvalues: bfloat16 [4, 8, 512, 512], P('seg', 'blk'), may hold values from 0.049804688 to 5
- back_weight: bfloat16 [4, 8, 512, 512], P('seg', 'blk'), may hold values from -0.25 to 0.25
- derivative: bfloat16 [4, 4, 32, 4096], P('seg', None, None, 'blk'), may hold values from 0 to 1
- query_acts: bfloat16 [4, 4, 32, 512], P('seg'), may hold values from -6 to 6
- query_top: bfloat16 [4, 32, 4096], P(None, None, 'blk'), may hold values from -0.0059814453 to 0.0059814453
Outputs:
- scores: float32 [4, 16], P(None, 'blk')
Inputs may be any that keep to these rules, and one draw needn't show every extreme that they name: In each pair of indices 2k and 2k+1 of blk one count is 2 and the other 1, so all counts add up to 12; slots below a device's count are valid. `basis_in`: each 512 x 512 matrix is orthogonal up to rounding. `basis_out`: each 512 x 512 matrix is orthogonal up to rounding.
All inputs are finite; a program needn't handle non-finite values.
Results may differ from a plain program's by a relative error of at most 0.015.
Values may be sent and summed in bfloat16 or wider, within the bound.
A program may use at most 64 MiB of HBM per device.

v0:
```python
import math
import jax
import jax.numpy as jnp
from jax import lax
from jax.sharding import PartitionSpec as P

TB = 64
SLOTS = 2
damping = 0.05


def passed_along(value, axis, steps):
    count = lax.axis_size(axis)
    first, last = (max(0, -steps), min(count, count - steps))
    return lax.ppermute(value, axis, [(source, source + steps) for source in range(first, last)])


def advance(current, weight, derivs):
    queries, query_tok, blk_width = current.shape
    mixed = jnp.dot(
        current.reshape(queries * query_tok, blk_width), weight, preferred_element_type=jnp.float32
    )
    mixed = mixed.reshape(queries, query_tok, blk_width)
    return (current.astype(jnp.float32) + mixed * derivs.astype(jnp.float32)).astype(jnp.bfloat16)


def precondition(current, acts_seg, inner_basis, outer_basis, eigen_block):
    queries, query_tok, blk_width = current.shape
    in_slices = inner_basis.shape[0]
    in_width = in_slices * blk_width
    rot_err = jnp.dot(
        current.reshape(queries * query_tok, blk_width),
        outer_basis,
        preferred_element_type=jnp.float32,
    )
    rot_err = rot_err.astype(jnp.bfloat16).reshape(queries, query_tok, blk_width)
    act_split = acts_seg.reshape(queries, query_tok, in_slices, blk_width)
    rot_acts = jnp.einsum(
        "qtid,ide->qtie", act_split, inner_basis, preferred_element_type=jnp.float32
    ).astype(jnp.bfloat16)
    core_raw = jnp.einsum("qtd,qtie->qdie", rot_err, rot_acts, preferred_element_type=jnp.float32)
    core_raw = core_raw.reshape(queries, blk_width, in_width)
    scaled_core = (core_raw / (eigen_block.astype(jnp.float32)[None] + damping)).astype(
        jnp.bfloat16
    )
    left_prod = jnp.einsum(
        "cd,qdf->qcf", outer_basis, scaled_core, preferred_element_type=jnp.float32
    ).astype(jnp.bfloat16)
    left_split = left_prod.reshape(queries, blk_width, in_slices, blk_width)
    precond = jnp.einsum(
        "qcie,ife->qcif", left_split, inner_basis, preferred_element_type=jnp.float32
    )
    return precond.astype(jnp.bfloat16).reshape(queries, blk_width, in_width)


def block_scores(grad_rows, act_rows, precond, slot_tokens):
    row_count = grad_rows.shape[0]
    group_count = max(row_count // slot_tokens, 1)
    group_rows = row_count // group_count
    batch_groups = math.gcd(group_count, 8)
    grad_groups = grad_rows.reshape(
        group_count // batch_groups, batch_groups, group_rows, grad_rows.shape[1]
    )
    act_groups = act_rows.reshape(
        group_count // batch_groups, batch_groups, group_rows, act_rows.shape[1]
    )

    def one_batch(operands):
        grad_block, act_block = operands
        outer_prod = jnp.einsum(
            "btd,bte->bde", grad_block, act_block, preferred_element_type=jnp.float32
        ).astype(jnp.bfloat16)
        return jnp.einsum("bde,qde->bq", outer_prod, precond, preferred_element_type=jnp.float32)

    partial_scores = lax.map(one_batch, (grad_groups, act_groups))
    return (partial_scores.reshape(group_count, precond.shape[0]), group_rows)


def body(
    train_acts,
    train_grads,
    counts,
    basis_in,
    basis_out,
    eigenvalues,
    back_weight,
    derivative,
    query_acts,
    query_top,
):
    seg_count = lax.axis_size("seg")
    seg_index = lax.axis_index("seg")
    blk_index = lax.axis_index("blk")
    n_slot = lax.axis_size("blk") * SLOTS
    slot_ids = jnp.arange(n_slot, dtype=jnp.int32)
    current = query_top
    for relay_step in range(seg_count - 1):
        moved = advance(current, back_weight[0, 0], derivative[0])
        arrived = passed_along(moved, "seg", -1)
        current = jnp.where(seg_index == seg_count - 2 - relay_step, arrived, current)
    precond = precondition(current, query_acts[0], basis_in[0], basis_out[0, 0], eigenvalues[0, 0])
    exchanged = lax.all_to_all(train_grads, "blk", split_axis=2, concat_axis=1, tiled=True)
    grad_rows = exchanged[0]
    scores_part, group_rows = block_scores(
        grad_rows, lax.all_gather(train_acts, "blk", axis=1, tiled=True)[0], precond, TB
    )
    slot_of = jnp.arange(scores_part.shape[0], dtype=jnp.int32) * group_rows // TB
    placement = (slot_of[:, None] == slot_ids[None, :]).astype(jnp.float32)
    local_scores = jnp.dot(scores_part.T, placement, precision=lax.Precision.HIGHEST)
    mine = lax.psum_scatter(local_scores, "blk", scatter_dimension=1, tiled=True)
    mine = lax.psum(mine, "seg")
    own_valid = (jnp.arange(SLOTS, dtype=jnp.int32) < counts[blk_index]).astype(jnp.float32)
    return mine * own_valid[None, :]


def solution(mesh):
    in_specs = (
        P("seg", "blk", None),
        P("seg", "blk", None),
        P(),
        P("seg", None, None, None),
        P("seg", "blk", None, None),
        P("seg", "blk", None, None),
        P("seg", "blk", None, None),
        P("seg", None, None, "blk"),
        P("seg", None, None, None),
        P(None, None, "blk"),
    )
    out_specs = P(None, "blk")
    return jax.shard_map(body, mesh=mesh, in_specs=in_specs, out_specs=out_specs, check_vma=False)
```

profile of v0, /device:TPU:0, one launch (start us, length us, event | category | flops | bytes accessed | tf_op | source)
XLA Modules:
  0.0 125.0 jit_solution(6837176893961638313)
XLA Ops:
  6.5 1.4 %fusion.15 = bf16[4,32,512]{2,1,0:T(8,128)(2,1)S(1)} fusion(bf16[4,32,512]{2,1,0:T(8,128)(2,1)} %param.21, bf16[1,1,512,512]{3,2,1,0:T(8,128)(2,1)} %param.18, bf16[1,4,32,512]{3,2,1,0:T(8,128)(2,1)} %param.19), kind=kOutput, calls=%fused_computation.20 | convolution fusion | flops 67436544 | bytes 917504 | tf_op jit(solution)/shard_map/dot_general | solution.py:20
  8.0 1.3 %collective-permute-start = (bf16[4,32,512]{2,1,0:T(8,128)(2,1)S(1)}, bf16[4,32,512]{2,1,0:T(8,128)(2,1)S(1)}, u32[]{:S(2)}, u32[]{:S(2)}) collective-permute-start(bf16[4,32,512]{2,1,0:T(8,128)(2,1)S(1)} %fusion.15), channel_id=1, source_target_pairs={{8,0},{16,8},{24,16},{9,1},{17,9},{25,17},{10,2},{18,10},{26,18},{... | collective-permute-start | bytes 393224 | tf_op jit(solution)/shard_map/ppermute | solution.py:15
  9.3 5.0 %copy.25 = bf16[1,128,4096]{1,0,2:T(2,128)(2,1)S(1)} copy(bf16[1,128,4096]{2,1,0:T(8,128)(2,1)} %param.13) | data formatting | bytes 2097152 | tf_op args[1]
  14.8 23.4 %reduce = bf16[4096,128]{1,0:T(8,128)(2,1)} reduce(bf16[4096,1,128]{2,1,0:T(2,128)(2,1)S(1)} %bitcast.92, bf16[]{:T(256)} %broadcast.63), dimensions={1}, to_apply=%bitcast.73.reduce_sub_computation | reduce | bytes 2097154
  38.2 2.2 %reshape.95 = bf16[8,2,32768]{2,1,0:T(2,128)(2,1)} reshape(bf16[4096,128]{1,0:T(8,128)(2,1)} %reduce) | data formatting | bytes 2097152
  40.4 5.3 %all-to-all-start = ((bf16[8,2,32768]{2,1,0:T(2,128)(2,1)}), bf16[8,2,32768]{2,1,0:T(2,128)(2,1)}, u32[]{:S(2)}, u32[]{:S(2)}) async-start(bf16[8,2,32768]{2,1,0:T(2,128)(2,1)} %reshape.95), calls=%async_computation | async-start | bytes 2097152 | tf_op jit(solution)/shard_map/all_to_all | solution.py:102
  46.9 1.3 %collective-permute-start.1 = (bf16[4,32,512]{2,1,0:T(8,128)(2,1)S(1)}, bf16[4,32,512]{2,1,0:T(8,128)(2,1)S(1)}, u32[]{:S(2)}, u32[]{:S(2)}) collective-permute-start(bf16[4,32,512]{2,1,0:T(8,128)(2,1)S(1)} %add_convert_fusion.1), channel_id=1, source_target_pairs={{8,0},{16,8},{24,16},{9,1},{17,9},{25,17},{10,2},{18,10},{26,18},{... | collective-permute-start | bytes 393224 | tf_op jit(solution)/shard_map/ppermute | solution.py:15
  48.3 7.2 %collective-permute-done.1 = bf16[4,32,512]{2,1,0:T(8,128)(2,1)S(1)} collective-permute-done((bf16[4,32,512]{2,1,0:T(8,128)(2,1)S(1)}, bf16[4,32,512]{2,1,0:T(8,128)(2,1)S(1)}, u32[]{:S(2)}, u32[]{:S(2)}) %collective-permute-start.1) | collective-permute-done | bytes 131104 | tf_op jit(solution)/shard_map/ppermute | solution.py:15
  55.8 1.5 %collective-permute-start.2 = (bf16[4,32,512]{2,1,0:T(8,128)(2,1)S(1)}, bf16[4,32,512]{2,1,0:T(8,128)(2,1)S(1)}, u32[]{:S(2)}, u32[]{:S(2)}) collective-permute-start(bf16[4,32,512]{2,1,0:T(8,128)(2,1)S(1)} %add_convert_fusion), channel_id=1, source_target_pairs={{8,0},{16,8},{24,16},{9,1},{17,9},{25,17},{10,2},{18,10},{26,18},{... | collective-permute-start | bytes 393224 | tf_op jit(solution)/shard_map/ppermute | solution.py:15
  57.3 1.3 %fusion.16 = bf16[4,32,512]{2,1,0:T(8,128)(2,1)S(1)} fusion(bf16[1,1,512,512]{3,2,1,0:T(8,128)(2,1)} %param.15, bf16[1,4,32,512]{3,2,1,0:T(8,128)(2,1)S(1)} %copy-done.7), kind=kOutput, calls=%fused_computation.21 | convolution fusion | flops 67174400 | bytes 786432 | tf_op jit(solution)/shard_map/qtid,ide->qtie/dot_general | solution.py:38
  60.5 2.7 %collective-permute-done.2 = bf16[4,32,512]{2,1,0:T(8,128)(2,1)S(1)} collective-permute-done((bf16[4,32,512]{2,1,0:T(8,128)(2,1)S(1)}, bf16[4,32,512]{2,1,0:T(8,128)(2,1)S(1)}, u32[]{:S(2)}, u32[]{:S(2)}) %collective-permute-start.2) | collective-permute-done | bytes 131104 | tf_op jit(solution)/shard_map/ppermute | solution.py:15
  63.5 3.2 %fusion.13 = bf16[4,512,512]{2,1,0:T(8,128)(2,1)} fusion(bf16[4,32,512]{2,1,0:T(8,128)(2,1)S(1)} %bitcast.96, bf16[4,32,512]{2,1,0:T(8,128)(2,1)S(1)} %fusion.16, f32[512,512]{1,0:T(8,128)S(1)} %add_bitcast_fusion, bf16[1,1,512,512]{3,2,1,0:T(8,128)(2,1)S(1)} %copy-done), kind=kOutput, calls=%fused_computation.13 | convolution fusion | flops 1142947840 | bytes 3932160 | tf_op jit(solution)/shard_map/cd,qdf->qcf/dot_general | solution.py:46
  66.7 2.9 %fusion.10 = bf16[4,512,512]{2,1,0:T(8,128)(2,1)S(1)} fusion(bf16[4,512,512]{2,1,0:T(8,128)(2,1)} %fusion.13, bf16[1,1,512,512]{3,2,1,0:T(8,128)(2,1)S(1)} %copy-done.6), kind=kOutput, calls=%fused_computation.12 | convolution fusion | flops 1074790400 | bytes 4718592 | tf_op jit(solution)/shard_map/qcie,ife->qcif/dot_general | solution.py:50
  69.6 3.0 %copy.29 = bf16[4,512,512]{2,0,1:T(4,128)(2,1)} copy(bf16[4,512,512]{2,1,0:T(8,128)(2,1)S(1)} %fusion.10) | data formatting | bytes 4194304 | tf_op jit(solution)/shard_map/while | solution.py:75
  72.5 4.3 %reshape.96 = bf16[4096,1,128]{2,1,0:T(2,128)(2,1)S(1)} reshape(bf16[8,2,32768]{2,1,0:T(2,128)(2,1)} %all-to-all-done) | data formatting | bytes 2097152
  76.9 1.1 copy.35
  78.0 1.5 %copy.26 = bf16[1,8,128,512]{3,2,1,0:T(8,128)(2,1)S(1)} copy(bf16[1,8,128,512]{2,3,1,0:T(8,128)(2,1)} %bitcast.94) | data formatting | bytes 2097152 | tf_op jit(solution)/shard_map/all_to_all | solution.py:102
  79.5 12.8 %while.10 = (s32[]{:T(128)}, f32[2,8,4]{1,0,2:T(2,128)S(1)}, bf16[2,8,64,512]{3,2,1,0:T(8,128)(2,1)S(1)}, bf16[2,8,64,512]{3,2,1,0:T(8,128)(2,1)}, bf16[4,512,512]{2,0,1:T(4,128)(2,1)}, /*index=5*/s32[]{:T(128)}, s32[]{:T(128)}) while((s32[]{:T(128)}, f32[2,8,4]{1,0,2:T(2,128)S(1)}, bf16[2,8,64,512]{3,2,1,0:T(8,128)(2,1)S(1)}, ...), condition=%wide.region_1.2_spmd, body=%wide.region_0.1_spmd.sunk | while | flops 287309824 | bytes 19924460 | solution.py:75
  79.5 2.5 %convolution_convert_fusion.4 = bf16[8,512,512]{2,1,0:T(8,128)(2,1)S(1)} fusion(bf16[2,8,64,512]{3,2,1,0:T(8,128)(2,1)} %get-tuple-element.111, s32[]{:T(128)} %get-tuple-element.101, bf16[2,8,64,512]{3,2,1,0:T(8,128)(2,1)S(1)} %get-tuple-element.110), kind=kOutput, calls=%fused_computation.2.clone.1 | convolution fusion | flops 270532608 | bytes 5243904 | tf_op jit(solution)/shard_map/while/body/eval_jaxpr/btd,bte->bde/dot_general | solution.py:70
  82.0 3.8 %fusion.47 = f32[8,4,1]{0,1,2:T(4,128)S(1)} fusion(bf16[4,512,512]{2,0,1:T(4,128)(2,1)S(1)} %copy-done.2, bf16[8,512,512]{2,1,0:T(8,128)(2,1)S(1)} %convolution_convert_fusion.4), kind=kOutput, calls=%fused_computation.clone.1 | convolution fusion | flops 16777216 | bytes 6291584 | tf_op jit(solution)/shard_map/while/body/eval_jaxpr/bde,qde->bq/dot_general | solution.py:73
  85.9 2.5 %convolution_convert_fusion.4 = bf16[8,512,512]{2,1,0:T(8,128)(2,1)S(1)} fusion(bf16[2,8,64,512]{3,2,1,0:T(8,128)(2,1)} %get-tuple-element.111, s32[]{:T(128)} %get-tuple-element.101, bf16[2,8,64,512]{3,2,1,0:T(8,128)(2,1)S(1)} %get-tuple-element.110), kind=kOutput, calls=%fused_computation.2.clone.1 | convolution fusion | flops 270532608 | bytes 5243904 | tf_op jit(solution)/shard_map/while/body/eval_jaxpr/btd,bte->bde/dot_general | solution.py:70
  88.4 3.8 %fusion.47 = f32[8,4,1]{0,1,2:T(4,128)S(1)} fusion(bf16[4,512,512]{2,0,1:T(4,128)(2,1)S(1)} %copy-done.2, bf16[8,512,512]{2,1,0:T(8,128)(2,1)S(1)} %convolution_convert_fusion.4), kind=kOutput, calls=%fused_computation.clone.1 | convolution fusion | flops 16777216 | bytes 6291584 | tf_op jit(solution)/shard_map/while/body/eval_jaxpr/bde,qde->bq/dot_general | solution.py:73
  92.6 13.1 %all-reduce = f32[4,16]{0,1:T(8,128)S(1)} all-reduce(f32[4,16]{0,1:T(8,128)S(1)} %fusion.29), channel_id=2, replica_groups=mesh['seg'=4,'blk'=8] {'blk'}, use_global_device_ids=true, to_apply=%region_2.3.clone | all-reduce | flops 64 | bytes 512
  106.4 11.2 %psum.7 = f32[4,2]{0,1:T(2,128)S(1)} all-reduce(f32[4,2]{0,1:T(2,128)S(1)} %constant_dynamic-slice_fusion), channel_id=1, replica_groups=mesh['seg'=4,'blk'=8] {'seg'}, use_global_device_ids=true, to_apply=%region_3.4 | all-reduce | flops 8 | bytes 64 | tf_op jit(solution)/shard_map/psum | solution.py:111
  (45 shorter events, 5.2 us)
Async XLA Ops:
  6.5 56.7 %copy-start = (bf16[1,1,512,512]{3,2,1,0:T(8,128)(2,1)S(1)}, bf16[1,1,512,512]{3,2,1,0:T(8,128)(2,1)}, u32[]{:S(2)}) copy-start(bf16[1,1,512,512]{3,2,1,0:T(8,128)(2,1)} %param.16) | copy-start | bytes 1572868
  8.0 38.5 %collective-permute-start = (bf16[4,32,512]{2,1,0:T(8,128)(2,1)S(1)}, bf16[4,32,512]{2,1,0:T(8,128)(2,1)S(1)}, u32[]{:S(2)}, u32[]{:S(2)}) collective-permute-start(bf16[4,32,512]{2,1,0:T(8,128)(2,1)S(1)} %fusion.15), channel_id=1, source_target_pairs={{8,0},{16,8},{24,16},{9,1},{17,9},{25,17},{10,2},{18,10},{26,18},{... | collective-permute-start | bytes 393224 | tf_op jit(solution)/shard_map/ppermute | solution.py:15
  38.2 8.3 %copy-start.5 = (bf16[4,32,512]{2,1,0:T(8,128)(2,1)S(1)}, bf16[4,32,512]{2,1,0:T(8,128)(2,1)}, u32[]{:S(2)}) copy-start(bf16[4,32,512]{2,1,0:T(8,128)(2,1)} %param.21) | copy-start | bytes 393220
  38.2 8.4 %copy-start.1 = (bf16[1,1,512,512]{3,2,1,0:T(8,128)(2,1)S(1)}, bf16[1,1,512,512]{3,2,1,0:T(8,128)(2,1)}, u32[]{:S(2)}) copy-start(bf16[1,1,512,512]{3,2,1,0:T(8,128)(2,1)} %param.18) | copy-start | bytes 1572868
  38.2 8.4 %copy-start.4 = (bf16[1,4,32,512]{3,2,1,0:T(8,128)(2,1)S(1)}, bf16[1,4,32,512]{3,2,1,0:T(8,128)(2,1)}, u32[]{:S(2)}) copy-start(bf16[1,4,32,512]{3,2,1,0:T(8,128)(2,1)} %param.19) | copy-start | bytes 393220
  40.4 7.7 %copy-start.3 = (bf16[1,1,512,512]{3,2,1,0:T(8,128)(2,1)S(1)}, bf16[1,1,512,512]{3,2,1,0:T(8,128)(2,1)}, u32[]{:S(2)}) copy-start(bf16[1,1,512,512]{3,2,1,0:T(8,128)(2,1)} %param.17) | copy-start | bytes 1572868
  40.4 32.1 %all-to-all-start = ((bf16[8,2,32768]{2,1,0:T(2,128)(2,1)}), bf16[8,2,32768]{2,1,0:T(2,128)(2,1)}, u32[]{:S(2)}, u32[]{:S(2)}) async-start(bf16[8,2,32768]{2,1,0:T(2,128)(2,1)} %reshape.95), calls=%async_computation | async-start | bytes 2097152 | tf_op jit(solution)/shard_map/all_to_all | solution.py:102
  45.8 11.5 %copy-start.7 = (bf16[1,4,32,512]{3,2,1,0:T(8,128)(2,1)S(1)}, bf16[1,4,32,512]{3,2,1,0:T(8,128)(2,1)}, u32[]{:S(2)}) copy-start(bf16[1,4,32,512]{3,2,1,0:T(8,128)(2,1)} %param.20) | copy-start | bytes 393220
  45.8 33.7 %all-gather.2.cloned.1.call-start = ((), (), s32[]{:S(2)}) async-start(), calls=%async_computation.1 | async-start | bytes 1179648 | tf_op jit(solution)/shard_map/all_gather | solution.py:105
  46.6 12.0 %copy-start.9 = (u32[32]{0:T(128)S(1)}, u32[32]{0:T(128)}, u32[]{:S(2)}) copy-start(u32[32]{0:T(128)} %constant.56) | copy-start | bytes 388
  46.6 13.3 %copy-start.8 = (s32[8]{0:T(128)S(1)}, s32[8]{0:T(128)}, u32[]{:S(2)}) copy-start(s32[8]{0:T(128)} %param.14) | copy-start | bytes 100
  46.9 8.7 %collective-permute-start.1 = (bf16[4,32,512]{2,1,0:T(8,128)(2,1)S(1)}, bf16[4,32,512]{2,1,0:T(8,128)(2,1)S(1)}, u32[]{:S(2)}, u32[]{:S(2)}) collective-permute-start(bf16[4,32,512]{2,1,0:T(8,128)(2,1)S(1)} %add_convert_fusion.1), channel_id=1, source_target_pairs={{8,0},{16,8},{24,16},{9,1},{17,9},{25,17},{10,2},{18,10},{26,18},{... | collective-permute-start | bytes 393224 | tf_op jit(solution)/shard_map/ppermute | solution.py:15
  55.8 7.4 %collective-permute-start.2 = (bf16[4,32,512]{2,1,0:T(8,128)(2,1)S(1)}, bf16[4,32,512]{2,1,0:T(8,128)(2,1)S(1)}, u32[]{:S(2)}, u32[]{:S(2)}) collective-permute-start(bf16[4,32,512]{2,1,0:T(8,128)(2,1)S(1)} %add_convert_fusion), channel_id=1, source_target_pairs={{8,0},{16,8},{24,16},{9,1},{17,9},{25,17},{10,2},{18,10},{26,18},{... | collective-permute-start | bytes 393224 | tf_op jit(solution)/shard_map/ppermute | solution.py:15
  63.5 3.2 %copy-start.6 = (bf16[1,1,512,512]{3,2,1,0:T(8,128)(2,1)S(1)}, bf16[1,1,512,512]{3,2,1,0:T(8,128)(2,1)}, u32[]{:S(2)}) copy-start(bf16[1,1,512,512]{3,2,1,0:T(8,128)(2,1)} %param.15) | copy-start | bytes 1572868
  79.5 2.5 %copy-start.2 = (bf16[4,512,512]{2,0,1:T(4,128)(2,1)S(1)}, bf16[4,512,512]{2,0,1:T(4,128)(2,1)}, u32[]{:S(2)}) copy-start(bf16[4,512,512]{2,0,1:T(4,128)(2,1)} %get-tuple-element.112) | copy-start | bytes 6291460 | tf_op jit(solution)/shard_map/while
  85.9 2.5 %copy-start.2 = (bf16[4,512,512]{2,0,1:T(4,128)(2,1)S(1)}, bf16[4,512,512]{2,0,1:T(4,128)(2,1)}, u32[]{:S(2)}) copy-start(bf16[4,512,512]{2,0,1:T(4,128)(2,1)} %get-tuple-element.112) | copy-start | bytes 6291460 | tf_op jit(solution)/shard_map/while
Sparse Core Ops, SparseCore 0:
  48.5 26.8 all-gather.1
where the time goes:
time: 126 us; the launch traced here: 125 us
  other arithmetic  24.9 us (20%)
  blocking collectives  24.2 us (19%)
  matrix products  22.4 us (18%)
  local copies, waits for them, and re-layouts  19.1 us (15%)
  between operations  14.3 us (11%)
  waiting for transfers between devices  10.6 us (8%)
  starting transfers between devices  9.43 us (7%)
    unnamed x1, other arithmetic  23.4 us
    unnamed x25, local copies, waits for them, and re-layouts  13.9 us
    unnamed x1, blocking collectives  13.1 us
    psum x1, blocking collectives, body(): mine = lax.psum(mine, 'seg')  11.2 us
    ppermute x3, waiting for transfers between devices, passed_along(): lax.ppermute(value, axis, [(source, source + steps) for source in range(f...  9.91 us
    dot_general x2, matrix products, one_batch(): jnp.einsum('bde,qde->bq', outer_prod, precond, preferred_element_type=jnp...  7.62 us
    all_to_all x1, starting transfers between devices, body(): lax.all_to_all(train_grads, 'blk', split_axis=2, concat_axis=1, tiled=True)  5.33 us
    dot_general x2, matrix products, one_batch(): jnp.einsum('btd,bte->bde', grad_block, act_block, preferred_element_type=...  4.98 us
  transfers between devices with their start and end apart: 5, of which 2 were waited for; matrix products, arithmetic and copies ran while one was open for 40% of the time, Pallas kernels for 0%

commit v1 on v0

--- a/solution.py
+++ b/solution.py
@@ -108,7 +108,7 @@
     placement = (slot_of[:, None] == slot_ids[None, :]).astype(jnp.float32)
     local_scores = jnp.dot(scores_part.T, placement, precision=lax.Precision.HIGHEST)
     mine = lax.psum_scatter(local_scores, "blk", scatter_dimension=1, tiled=True)
-    mine = lax.psum(mine, "seg")
+    mine = jnp.sum(lax.all_gather(mine, "seg"), axis=0)
     own_valid = (jnp.arange(SLOTS, dtype=jnp.int32) < counts[blk_index]).astype(jnp.float32)
     return mine * own_valid[None, :]
 

time: 126 us -> 125 us (level)
    psum x1 -> x0, blocking collectives: 11.2 us -> none  [body(): mine = lax.psum(mine, 'seg')]
    all_gather x0 -> x1, blocking collectives: none -> 10.4 us  [body(): mine = jnp.sum(lax.all_gather(mine, 'seg'), axis=0)]
  transfers between devices with their start and end apart: 5 -> 5, of which waited for: 2 -> 2; matrix products, arithmetic and copies ran while one was open for 40% -> 41% of each run, Pallas kernels for 0% -> 0%
where the time goes in v1:
time: 125 us; the launch traced here: 124 us
  other arithmetic  24.9 us (20%)
  blocking collectives  23.4 us (19%)
  matrix products  22.4 us (18%)
  local copies, waits for them, and re-layouts  19.1 us (15%)
  between operations  14.3 us (11%)
  waiting for transfers between devices  10.6 us (8%)
  starting transfers between devices  9.43 us (8%)
    unnamed x1, other arithmetic  23.4 us
    unnamed x25, local copies, waits for them, and re-layouts  13.9 us
    unnamed x1, blocking collectives  13.1 us
    all_gather x1, blocking collectives, body(): mine = jnp.sum(lax.all_gather(mine, 'seg'), axis=0)  10.4 us
    ppermute x3, waiting for transfers between devices, passed_along(): lax.ppermute(value, axis, [(source, source + steps) for source in range(f...  9.91 us
    dot_general x2, matrix products, one_batch(): jnp.einsum('bde,qde->bq', outer_prod, precond, preferred_element_type=jnp...  7.62 us
    all_to_all x1, starting transfers between devices, body(): lax.all_to_all(train_grads, 'blk', split_axis=2, concat_axis=1, tiled=True)  5.33 us
    dot_general x2, matrix products, one_batch(): jnp.einsum('btd,bte->bde', grad_block, act_block, preferred_element_type=...  4.98 us
  transfers between devices with their start and end apart: 5, of which 2 were waited for; matrix products, arithmetic and copies ran while one was open for 41% of the time, Pallas kernels for 0%

profile of v1, /device:TPU:0, one launch (start us, length us, event | category | flops | bytes accessed | tf_op | source)
XLA Modules:
  0.0 124.2 jit_solution(12554309127313614516)
XLA Ops:
  6.5 1.4 %fusion.15 = bf16[4,32,512]{2,1,0:T(8,128)(2,1)S(1)} fusion(bf16[4,32,512]{2,1,0:T(8,128)(2,1)} %param.21, bf16[1,1,512,512]{3,2,1,0:T(8,128)(2,1)} %param.18, bf16[1,4,32,512]{3,2,1,0:T(8,128)(2,1)} %param.19), kind=kOutput, calls=%fused_computation.20 | convolution fusion | flops 67436544 | bytes 917504 | tf_op jit(solution)/shard_map/dot_general | solution.py:20
  8.0 1.3 %collective-permute-start = (bf16[4,32,512]{2,1,0:T(8,128)(2,1)S(1)}, bf16[4,32,512]{2,1,0:T(8,128)(2,1)S(1)}, u32[]{:S(2)}, u32[]{:S(2)}) collective-permute-start(bf16[4,32,512]{2,1,0:T(8,128)(2,1)S(1)} %fusion.15), channel_id=1, source_target_pairs={{8,0},{16,8},{24,16},{9,1},{17,9},{25,17},{10,2},{18,10},{26,18},{... | collective-permute-start | bytes 393224 | tf_op jit(solution)/shard_map/ppermute | solution.py:15
  9.3 5.0 %copy.25 = bf16[1,128,4096]{1,0,2:T(2,128)(2,1)S(1)} copy(bf16[1,128,4096]{2,1,0:T(8,128)(2,1)} %param.13) | data formatting | bytes 2097152 | tf_op args[1]
  14.8 23.4 %reduce.1 = bf16[4096,128]{1,0:T(8,128)(2,1)} reduce(bf16[4096,1,128]{2,1,0:T(2,128)(2,1)S(1)} %bitcast.94, bf16[]{:T(256)} %broadcast.63), dimensions={1}, to_apply=%bitcast.75.reduce_sub_computation | reduce | bytes 2097154
  38.2 2.2 %reshape.99 = bf16[8,2,32768]{2,1,0:T(2,128)(2,1)} reshape(bf16[4096,128]{1,0:T(8,128)(2,1)} %reduce.1) | data formatting | bytes 2097152
  40.4 5.3 %all-to-all-start = ((bf16[8,2,32768]{2,1,0:T(2,128)(2,1)}), bf16[8,2,32768]{2,1,0:T(2,128)(2,1)}, u32[]{:S(2)}, u32[]{:S(2)}) async-start(bf16[8,2,32768]{2,1,0:T(2,128)(2,1)} %reshape.99), calls=%async_computation | async-start | bytes 2097152 | tf_op jit(solution)/shard_map/all_to_all | solution.py:102
  46.9 1.3 %collective-permute-start.1 = (bf16[4,32,512]{2,1,0:T(8,128)(2,1)S(1)}, bf16[4,32,512]{2,1,0:T(8,128)(2,1)S(1)}, u32[]{:S(2)}, u32[]{:S(2)}) collective-permute-start(bf16[4,32,512]{2,1,0:T(8,128)(2,1)S(1)} %add_convert_fusion.1), channel_id=1, source_target_pairs={{8,0},{16,8},{24,16},{9,1},{17,9},{25,17},{10,2},{18,10},{26,18},{... | collective-permute-start | bytes 393224 | tf_op jit(solution)/shard_map/ppermute | solution.py:15
  48.3 7.2 %collective-permute-done.1 = bf16[4,32,512]{2,1,0:T(8,128)(2,1)S(1)} collective-permute-done((bf16[4,32,512]{2,1,0:T(8,128)(2,1)S(1)}, bf16[4,32,512]{2,1,0:T(8,128)(2,1)S(1)}, u32[]{:S(2)}, u32[]{:S(2)}) %collective-permute-start.1) | collective-permute-done | bytes 131104 | tf_op jit(solution)/shard_map/ppermute | solution.py:15
  55.8 1.5 %collective-permute-start.2 = (bf16[4,32,512]{2,1,0:T(8,128)(2,1)S(1)}, bf16[4,32,512]{2,1,0:T(8,128)(2,1)S(1)}, u32[]{:S(2)}, u32[]{:S(2)}) collective-permute-start(bf16[4,32,512]{2,1,0:T(8,128)(2,1)S(1)} %add_convert_fusion), channel_id=1, source_target_pairs={{8,0},{16,8},{24,16},{9,1},{17,9},{25,17},{10,2},{18,10},{26,18},{... | collective-permute-start | bytes 393224 | tf_op jit(solution)/shard_map/ppermute | solution.py:15
  57.3 1.3 %fusion.16 = bf16[4,32,512]{2,1,0:T(8,128)(2,1)S(1)} fusion(bf16[1,1,512,512]{3,2,1,0:T(8,128)(2,1)} %param.15, bf16[1,4,32,512]{3,2,1,0:T(8,128)(2,1)S(1)} %copy-done.7), kind=kOutput, calls=%fused_computation.21 | convolution fusion | flops 67174400 | bytes 786432 | tf_op jit(solution)/shard_map/qtid,ide->qtie/dot_general | solution.py:38
  60.5 2.7 %collective-permute-done.2 = bf16[4,32,512]{2,1,0:T(8,128)(2,1)S(1)} collective-permute-done((bf16[4,32,512]{2,1,0:T(8,128)(2,1)S(1)}, bf16[4,32,512]{2,1,0:T(8,128)(2,1)S(1)}, u32[]{:S(2)}, u32[]{:S(2)}) %collective-permute-start.2) | collective-permute-done | bytes 131104 | tf_op jit(solution)/shard_map/ppermute | solution.py:15
  63.5 3.2 %fusion.13 = bf16[4,512,512]{2,1,0:T(8,128)(2,1)} fusion(bf16[4,32,512]{2,1,0:T(8,128)(2,1)S(1)} %bitcast.98, bf16[4,32,512]{2,1,0:T(8,128)(2,1)S(1)} %fusion.16, f32[512,512]{1,0:T(8,128)S(1)} %add_bitcast_fusion, bf16[1,1,512,512]{3,2,1,0:T(8,128)(2,1)S(1)} %copy-done), kind=kOutput, calls=%fused_computation.13 | convolution fusion | flops 1142947840 | bytes 3932160 | tf_op jit(solution)/shard_map/cd,qdf->qcf/dot_general | solution.py:46
  66.7 2.9 %fusion.10 = bf16[4,512,512]{2,1,0:T(8,128)(2,1)S(1)} fusion(bf16[4,512,512]{2,1,0:T(8,128)(2,1)} %fusion.13, bf16[1,1,512,512]{3,2,1,0:T(8,128)(2,1)S(1)} %copy-done.6), kind=kOutput, calls=%fused_computation.12 | convolution fusion | flops 1074790400 | bytes 4718592 | tf_op jit(solution)/shard_map/qcie,ife->qcif/dot_general | solution.py:50
  69.6 3.0 %copy.29 = bf16[4,512,512]{2,0,1:T(4,128)(2,1)} copy(bf16[4,512,512]{2,1,0:T(8,128)(2,1)S(1)} %fusion.10) | data formatting | bytes 4194304 | tf_op jit(solution)/shard_map/while | solution.py:75
  72.5 4.3 %reshape.100 = bf16[4096,1,128]{2,1,0:T(2,128)(2,1)S(1)} reshape(bf16[8,2,32768]{2,1,0:T(2,128)(2,1)} %all-to-all-done) | data formatting | bytes 2097152
  76.9 1.1 copy.35
  78.0 1.5 %copy.26 = bf16[1,8,128,512]{3,2,1,0:T(8,128)(2,1)S(1)} copy(bf16[1,8,128,512]{2,3,1,0:T(8,128)(2,1)} %bitcast.96) | data formatting | bytes 2097152 | tf_op jit(solution)/shard_map/all_to_all | solution.py:102
  79.5 12.8 %while.10 = (s32[]{:T(128)}, f32[2,8,4]{1,0,2:T(2,128)S(1)}, bf16[2,8,64,512]{3,2,1,0:T(8,128)(2,1)S(1)}, bf16[2,8,64,512]{3,2,1,0:T(8,128)(2,1)}, bf16[4,512,512]{2,0,1:T(4,128)(2,1)}, /*index=5*/s32[]{:T(128)}, s32[]{:T(128)}) while((s32[]{:T(128)}, f32[2,8,4]{1,0,2:T(2,128)S(1)}, bf16[2,8,64,512]{3,2,1,0:T(8,128)(2,1)S(1)}, ...), condition=%wide.region_1.2_spmd, body=%wide.region_0.1_spmd.sunk | while | flops 287309824 | bytes 19924460 | solution.py:75
  79.5 2.5 %convolution_convert_fusion.4 = bf16[8,512,512]{2,1,0:T(8,128)(2,1)S(1)} fusion(bf16[2,8,64,512]{3,2,1,0:T(8,128)(2,1)} %get-tuple-element.111, s32[]{:T(128)} %get-tuple-element.101, bf16[2,8,64,512]{3,2,1,0:T(8,128)(2,1)S(1)} %get-tuple-element.110), kind=kOutput, calls=%fused_computation.2.clone.1 | convolution fusion | flops 270532608 | bytes 5243904 | tf_op jit(solution)/shard_map/while/body/eval_jaxpr/btd,bte->bde/dot_general | solution.py:70
  82.0 3.8 %fusion.47 = f32[8,4,1]{0,1,2:T(4,128)S(1)} fusion(bf16[4,512,512]{2,0,1:T(4,128)(2,1)S(1)} %copy-done.2, bf16[8,512,512]{2,1,0:T(8,128)(2,1)S(1)} %convolution_convert_fusion.4), kind=kOutput, calls=%fused_computation.clone.1 | convolution fusion | flops 16777216 | bytes 6291584 | tf_op jit(solution)/shard_map/while/body/eval_jaxpr/bde,qde->bq/dot_general | solution.py:73
  85.9 2.5 %convolution_convert_fusion.4 = bf16[8,512,512]{2,1,0:T(8,128)(2,1)S(1)} fusion(bf16[2,8,64,512]{3,2,1,0:T(8,128)(2,1)} %get-tuple-element.111, s32[]{:T(128)} %get-tuple-element.101, bf16[2,8,64,512]{3,2,1,0:T(8,128)(2,1)S(1)} %get-tuple-element.110), kind=kOutput, calls=%fused_computation.2.clone.1 | convolution fusion | flops 270532608 | bytes 5243904 | tf_op jit(solution)/shard_map/while/body/eval_jaxpr/btd,bte->bde/dot_general | solution.py:70
  88.4 3.8 %fusion.47 = f32[8,4,1]{0,1,2:T(4,128)S(1)} fusion(bf16[4,512,512]{2,0,1:T(4,128)(2,1)S(1)} %copy-done.2, bf16[8,512,512]{2,1,0:T(8,128)(2,1)S(1)} %convolution_convert_fusion.4), kind=kOutput, calls=%fused_computation.clone.1 | convolution fusion | flops 16777216 | bytes 6291584 | tf_op jit(solution)/shard_map/while/body/eval_jaxpr/bde,qde->bq/dot_general | solution.py:73
  92.6 13.1 %all-reduce = f32[4,16]{0,1:T(8,128)S(1)} all-reduce(f32[4,16]{0,1:T(8,128)S(1)} %fusion.29), channel_id=3, replica_groups=mesh['seg'=4,'blk'=8] {'blk'}, use_global_device_ids=true, to_apply=%region_2.3.clone | all-reduce | flops 64 | bytes 512
  106.4 10.4 %all-gather.1 = f32[4,4,2]{1,2,0:T(2,128)S(1)} all-gather(f32[1,4,2]{1,2,0:T(2,128)S(1)} %dynamic-slice_bitcast_fusion), channel_id=2, replica_groups=mesh['seg'=4,'blk'=8] {'seg'}, dimensions={0}, use_global_device_ids=true | all-gather | bytes 160 | tf_op jit(solution)/shard_map/all_gather | solution.py:111
  (46 shorter events, 5.2 us)
Async XLA Ops:
  6.5 56.7 %copy-start = (bf16[1,1,512,512]{3,2,1,0:T(8,128)(2,1)S(1)}, bf16[1,1,512,512]{3,2,1,0:T(8,128)(2,1)}, u32[]{:S(2)}) copy-start(bf16[1,1,512,512]{3,2,1,0:T(8,128)(2,1)} %param.16) | copy-start | bytes 1572868
  8.0 38.5 %collective-permute-start = (bf16[4,32,512]{2,1,0:T(8,128)(2,1)S(1)}, bf16[4,32,512]{2,1,0:T(8,128)(2,1)S(1)}, u32[]{:S(2)}, u32[]{:S(2)}) collective-permute-start(bf16[4,32,512]{2,1,0:T(8,128)(2,1)S(1)} %fusion.15), channel_id=1, source_target_pairs={{8,0},{16,8},{24,16},{9,1},{17,9},{25,17},{10,2},{18,10},{26,18},{... | collective-permute-start | bytes 393224 | tf_op jit(solution)/shard_map/ppermute | solution.py:15
  38.2 8.3 %copy-start.5 = (bf16[4,32,512]{2,1,0:T(8,128)(2,1)S(1)}, bf16[4,32,512]{2,1,0:T(8,128)(2,1)}, u32[]{:S(2)}) copy-start(bf16[4,32,512]{2,1,0:T(8,128)(2,1)} %param.21) | copy-start | bytes 393220
  38.2 8.4 %copy-start.1 = (bf16[1,1,512,512]{3,2,1,0:T(8,128)(2,1)S(1)}, bf16[1,1,512,512]{3,2,1,0:T(8,128)(2,1)}, u32[]{:S(2)}) copy-start(bf16[1,1,512,512]{3,2,1,0:T(8,128)(2,1)} %param.18) | copy-start | bytes 1572868
  38.2 8.4 %copy-start.4 = (bf16[1,4,32,512]{3,2,1,0:T(8,128)(2,1)S(1)}, bf16[1,4,32,512]{3,2,1,0:T(8,128)(2,1)}, u32[]{:S(2)}) copy-start(bf16[1,4,32,512]{3,2,1,0:T(8,128)(2,1)} %param.19) | copy-start | bytes 393220
  40.4 7.7 %copy-start.3 = (bf16[1,1,512,512]{3,2,1,0:T(8,128)(2,1)S(1)}, bf16[1,1,512,512]{3,2,1,0:T(8,128)(2,1)}, u32[]{:S(2)}) copy-start(bf16[1,1,512,512]{3,2,1,0:T(8,128)(2,1)} %param.17) | copy-start | bytes 1572868
  40.4 32.1 %all-to-all-start = ((bf16[8,2,32768]{2,1,0:T(2,128)(2,1)}), bf16[8,2,32768]{2,1,0:T(2,128)(2,1)}, u32[]{:S(2)}, u32[]{:S(2)}) async-start(bf16[8,2,32768]{2,1,0:T(2,128)(2,1)} %reshape.99), calls=%async_computation | async-start | bytes 2097152 | tf_op jit(solution)/shard_map/all_to_all | solution.py:102
  45.8 11.5 %copy-start.7 = (bf16[1,4,32,512]{3,2,1,0:T(8,128)(2,1)S(1)}, bf16[1,4,32,512]{3,2,1,0:T(8,128)(2,1)}, u32[]{:S(2)}) copy-start(bf16[1,4,32,512]{3,2,1,0:T(8,128)(2,1)} %param.20) | copy-start | bytes 393220
  45.8 33.7 %all-gather.4.cloned.1.call-start = ((), (), s32[]{:S(2)}) async-start(), calls=%async_computation.1 | async-start | bytes 1179648 | tf_op jit(solution)/shard_map/all_gather | solution.py:105
  46.6 12.0 %copy-start.9 = (u32[32]{0:T(128)S(1)}, u32[32]{0:T(128)}, u32[]{:S(2)}) copy-start(u32[32]{0:T(128)} %constant.57) | copy-start | bytes 388
  46.6 13.3 %copy-start.8 = (s32[8]{0:T(128)S(1)}, s32[8]{0:T(128)}, u32[]{:S(2)}) copy-start(s32[8]{0:T(128)} %param.14) | copy-start | bytes 100
  46.9 8.7 %collective-permute-start.1 = (bf16[4,32,512]{2,1,0:T(8,128)(2,1)S(1)}, bf16[4,32,512]{2,1,0:T(8,128)(2,1)S(1)}, u32[]{:S(2)}, u32[]{:S(2)}) collective-permute-start(bf16[4,32,512]{2,1,0:T(8,128)(2,1)S(1)} %add_convert_fusion.1), channel_id=1, source_target_pairs={{8,0},{16,8},{24,16},{9,1},{17,9},{25,17},{10,2},{18,10},{26,18},{... | collective-permute-start | bytes 393224 | tf_op jit(solution)/shard_map/ppermute | solution.py:15
  55.8 7.4 %collective-permute-start.2 = (bf16[4,32,512]{2,1,0:T(8,128)(2,1)S(1)}, bf16[4,32,512]{2,1,0:T(8,128)(2,1)S(1)}, u32[]{:S(2)}, u32[]{:S(2)}) collective-permute-start(bf16[4,32,512]{2,1,0:T(8,128)(2,1)S(1)} %add_convert_fusion), channel_id=1, source_target_pairs={{8,0},{16,8},{24,16},{9,1},{17,9},{25,17},{10,2},{18,10},{26,18},{... | collective-permute-start | bytes 393224 | tf_op jit(solution)/shard_map/ppermute | solution.py:15
  63.5 3.2 %copy-start.6 = (bf16[1,1,512,512]{3,2,1,0:T(8,128)(2,1)S(1)}, bf16[1,1,512,512]{3,2,1,0:T(8,128)(2,1)}, u32[]{:S(2)}) copy-start(bf16[1,1,512,512]{3,2,1,0:T(8,128)(2,1)} %param.15) | copy-start | bytes 1572868
  79.5 2.5 %copy-start.2 = (bf16[4,512,512]{2,0,1:T(4,128)(2,1)S(1)}, bf16[4,512,512]{2,0,1:T(4,128)(2,1)}, u32[]{:S(2)}) copy-start(bf16[4,512,512]{2,0,1:T(4,128)(2,1)} %get-tuple-element.112) | copy-start | bytes 6291460 | tf_op jit(solution)/shard_map/while
  85.9 2.5 %copy-start.2 = (bf16[4,512,512]{2,0,1:T(4,128)(2,1)S(1)}, bf16[4,512,512]{2,0,1:T(4,128)(2,1)}, u32[]{:S(2)}) copy-start(bf16[4,512,512]{2,0,1:T(4,128)(2,1)} %get-tuple-element.112) | copy-start | bytes 6291460 | tf_op jit(solution)/shard_map/while
Sparse Core Ops, SparseCore 0:
  48.5 26.8 all-gather.3
